TPU v7x, 32 devices: a whole 2x2x4 slice. The times are simulated.
32 devices in a mesh: seq: 4 (over x, core), dp: 8 (over z, y).
Axes of the slice: x: 2, y: 2, z: 4, core: 2. Of those that a mesh axis runs over, the one named last changes fastest.
Arguments:
- tokens: bfloat16 [8, 2048, 2048], P('dp', 'seq'), may hold values from -6 to 6
- log_decay: float32 [8, 8, 2048], P('dp', None, 'seq'), may hold values from -1 to 0
- w_qkv: bfloat16 [2048, 3072], P('dp'), may hold values from -0.125 to 0.125
- w_gate: bfloat16 [2048, 1024], P('dp'), may hold values from -0.125 to 0.125
- w_out: bfloat16 [1024, 2048], P('dp'), may hold values from -0.1875 to 0.1875
- norm_gain: float32 [1024], replicated, may hold values from 0.1 to 1.9
Outputs:
- mixed_rows: bfloat16 [8, 2048, 2048], P('dp', 'seq')
All inputs are finite; a program needn't handle non-finite values.
Results may differ from a plain program's by a relative error of at most 0.0065.
Values may be sent and summed in bfloat16 or wider, within the bound.
A program may use at most 64 MiB of HBM per device.

v0:
```python
import jax
import jax.numpy as jnp
from jax import lax
from jax.sharding import PartitionSpec as P


def fold_states(carried, piece, before, block_totals, my_index):
    span = piece.shape[0]
    mine = lax.dynamic_index_in_dim(before, my_index, 0, keepdims=False)
    order = jnp.arange(span, dtype=jnp.int32)
    earlier = (order < my_index)[:, None]
    decay_gap = mine[None, :] - before - block_totals
    factor = jnp.where(earlier, jnp.exp(jnp.where(earlier, decay_gap, 0.0)), 0.0)
    return carried + jnp.einsum("jh,jhde->hde", factor, piece, precision=lax.Precision.HIGHEST)


def body(tokens, log_decay, w_qkv, w_gate, w_out, norm_gain):
    tok_rows = tokens[0]
    tok_count = tok_rows.shape[0]
    head_count = log_decay.shape[1]
    feat_count = norm_gain.shape[0]
    head_dim = feat_count // head_count
    seq_count = lax.axis_size("seq")
    seq_index = lax.axis_index("seq")
    qkv_width = w_qkv.shape[1] // seq_count
    gate_width = w_gate.shape[1] // seq_count
    slab_width = qkv_width + gate_width
    qkv_slab = lax.dynamic_slice_in_dim(w_qkv, seq_index * qkv_width, qkv_width, 1)
    gate_slab = lax.dynamic_slice_in_dim(w_gate, seq_index * gate_width, gate_width, 1)
    column_slab = jnp.concatenate([qkv_slab, gate_slab], axis=1)
    full_rows = lax.all_gather(column_slab, "dp", axis=0, tiled=True)
    piece = lax.all_gather(full_rows, "seq", axis=1, tiled=True)
    slab_count = piece.shape[1] // slab_width
    product = jnp.dot(tok_rows, piece, preferred_element_type=jnp.float32).reshape(
        tok_count, slab_count, slab_width
    )
    qkv_total = product[:, :, :qkv_width]
    gate_total = product[:, :, qkv_width:]
    projected = qkv_total.reshape(tok_count, seq_count * qkv_width)
    gate_pre = gate_total.reshape(tok_count, seq_count * gate_width)
    activated = (
        jax.nn.silu(projected).astype(jnp.bfloat16).reshape(tok_count, 3, head_count, head_dim)
    )
    query_rows = activated[:, 0]
    key_rows = activated[:, 1]
    value_rows = activated[:, 2]
    cum_decay = jnp.cumsum(log_decay[0], axis=1)
    block_decay = cum_decay[:, -1]
    key_factor = jnp.exp(block_decay[:, None] - cum_decay).T
    scaled_key = (key_rows.astype(jnp.float32) * key_factor[:, :, None]).astype(jnp.bfloat16)
    local_state = jnp.einsum(
        "thd,the->hde", scaled_key, value_rows, preferred_element_type=jnp.float32
    )
    my_index = lax.axis_index("seq")
    empty_state = jnp.zeros((head_count, head_dim, head_dim), jnp.float32)
    all_states, all_decays = (
        lax.all_gather(local_state[None].astype(jnp.bfloat16), "seq", axis=0, tiled=True).astype(
            jnp.float32
        ),
        lax.all_gather(block_decay[None].astype(jnp.bfloat16), "seq", axis=0, tiled=True).astype(
            jnp.float32
        ),
    )
    before = jnp.cumsum(all_decays, axis=0) - all_decays
    carried = fold_states(empty_state, all_states, before, all_decays, my_index)
    scores = jnp.einsum("thd,shd->hts", query_rows, key_rows, preferred_element_type=jnp.float32)
    positions = jnp.arange(tok_count, dtype=jnp.int32)
    causal_mask = (positions[None, :] <= positions[:, None])[None, :, :]
    decay_gap = cum_decay[:, :, None] - cum_decay[:, None, :]
    decay_mat = jnp.where(causal_mask, jnp.exp(jnp.where(causal_mask, decay_gap, 0.0)), 0.0)
    weighted = (scores * decay_mat).astype(jnp.bfloat16)
    intra_part = jnp.einsum(
        "hts,shd->thd", weighted, value_rows, preferred_element_type=jnp.float32
    )
    query_scaled = query_rows.astype(jnp.float32) * jnp.exp(cum_decay).T[:, :, None]
    inter_part = jnp.einsum("thd,hde->the", query_scaled, carried, precision=lax.Precision.HIGHEST)
    attended = (intra_part + inter_part).reshape(tok_count, feat_count)
    mean_square = jnp.mean(attended * attended, axis=1, keepdims=True)
    normed = attended * lax.rsqrt(mean_square + 1e-06) * norm_gain
    gated = (normed * jax.nn.sigmoid(gate_pre)).astype(jnp.bfloat16)
    out_sum = jnp.dot(
        gated, lax.all_gather(w_out, "dp", axis=0, tiled=True), preferred_element_type=jnp.float32
    )
    return out_sum.astype(jnp.bfloat16)[None]


def solution(mesh):
    placed = (
        P("dp", "seq", None),
        P("dp", None, "seq"),
        P("dp", None),
        P("dp", None),
        P("dp", None),
        P(),
    )
    return jax.shard_map(
        body, mesh=mesh, in_specs=placed, out_specs=P("dp", "seq", None), check_vma=False
    )
```

profile of v0, /device:TPU:0, one launch (start us, length us, event | category | flops | bytes accessed | tf_op | source)
XLA Modules:
  0.0 327.2 jit_solution(16576440834460175521)
XLA Ops:
  6.5 1.2 constant_dynamic-slice_fusion.2
  7.7 0.9 constant_dynamic-slice_fusion.1
  8.7 0.9 pad_maximum_fusion
  9.6 75.6 %all-gather.7.cloned.1.call-done = bf16[2048,1024]{1,0:T(8,128)(2,1)} async-done(((bf16[256,1024]{1,0:T(8,128)(2,1)}), bf16[2048,1024]{1,0:T(8,128)(2,1)}) %all-gather.7.cloned.1.call-update) | async-done | bytes 4194320 | tf_op jit(solution)/shard_map/all_gather | solution.py:31
  85.3 1.1 reduce-window.6
  87.0 104.2 %all-gather.9.cloned.1.call-done = bf16[2048,4096]{1,0:T(8,128)(2,1)} async-done(((bf16[2048,1024]{1,0:T(8,128)(2,1)}), bf16[2048,4096]{1,0:T(8,128)(2,1)}) %all-gather.9.cloned.1.call-update) | async-done | bytes 16777232 | tf_op jit(solution)/shard_map/all_gather | solution.py:32
  191.2 11.7 %fusion.12 = f32[4096,512]{1,0:T(8,128)S(1)} fusion(bf16[2048,4096]{1,0:T(8,128)(2,1)} %all-gather.9.cloned.1.call-done, bf16[1,512,2048]{2,1,0:T(8,128)(2,1)S(1)} %copy-done), kind=kOutput, calls=%fused_computation.17 | convolution fusion | flops 8589934592 | bytes 27262976 | tf_op jit(solution)/shard_map/dot_general | solution.py:34
  203.0 3.8 %slice.32 = f32[512,4,768]{0,2,1:T(8,128)} slice(f32[512,4,1024]{0,2,1:T(8,128)S(1)} %bitcast.65), slice={[0:512], [0:4], [0:768]} | slice | bytes 12582912 | tf_op jit(solution)/shard_map/slice | solution.py:37
  206.8 1.3 copy-done.1
  208.1 6.6 %copy.22 = f32[512,3,8,128]{3,0,2,1:T(8,128)} copy(f32[512,3,8,128]{0,3,2,1:T(8,128)} %bitcast.64) | data formatting | bytes 12582912 | tf_op jit(solution)/shard_map/reshape | solution.py:39
  214.7 4.4 %multiply_convert_fusion.1 = bf16[512,3,8,128]{3,0,2,1:T(8,128)(2,1)S(1)} fusion(f32[512,3,8,128]{3,0,2,1:T(8,128)} %copy.22), kind=kLoop, calls=%fused_computation.1 | loop fusion | flops 7864320 | bytes 9437184 | tf_op jit(solution)/shard_map/convert_element_type | solution.py:42
  219.1 1.7 copy-done.3
  220.8 2.3 convolution_convert_fusion.1
  223.2 0.5 all-gather.11.cloned.1.call-update
  223.7 0.6 dynamic-slice
  225.1 0.2 dynamic-update-slice
  225.4 6.1 %all-reduce = bf16[32]{0:T(256)(128)(2,1)S(1)} all-reduce(bf16[32]{0:T(256)(128)(2,1)S(1)} %dynamic-update-slice), channel_id=2, replica_groups=mesh['seq'=4,'dp'=8] {'seq'}, use_global_device_ids=true, to_apply=%add | all-reduce | flops 32 | bytes 128
  231.8 3.5 %fusion.7 = f32[512,4,256]{0,2,1:T(8,128)} fusion(f32[512,4,1024]{0,2,1:T(8,128)} %bitcast.66), kind=kLoop, calls=%fused_computation.10 | loop fusion | flops 1572864 | bytes 4194304 | tf_op jit(solution)/shard_map/div | solution.py:80
  235.2 6.7 %fusion = f32[8,128,512]{2,1,0:T(8,128)} fusion(f32[8,512]{1,0:T(8,128)S(1)} %get-tuple-element.6, pred[512,512]{1,0:T(8,128)(4,1)S(1)} %iota_compare_fusion, bf16[512,3,8,128]{3,0,2,1:T(8,128)(2,1)} %copy-done.3), kind=kOutput, calls=%fused_computation.2 | convolution fusion | flops 1084227584 | bytes 5537792 | tf_op jit(solution)/shard_map/hts,shd->thd/dot_general | solution.py:72
  242.0 1.6 multiply_reduce_fusion
  243.6 4.8 %fusion.11 = (f32[512]{0:T(512)S(1)}, f32[8,128,512]{2,1,0:T(8,128)S(1)}) fusion(f32[8,128,512]{2,1,0:T(8,128)} %fusion, f32[8,128,128]{2,1,0:T(8,128)S(1)} %multiply_reduce_fusion, f32[512,8]{0,1:T(8,128)S(1)} %get-tuple-element.5, bf16[512,3,8,128]{3,0,2,1:T(8,128)(2,1)} %copy-done.3), kind=kOutput, calls=%fused_computation.16 | convolution fusion | flops 807927296 | bytes 5785600 | tf_op jit(solution)/shard_map/thd,hde->the/dot_general | solution.py:76
  248.4 0.3 fusion.10
  248.7 66.0 %all-gather.11.cloned.1.call-done = bf16[1024,2048]{1,0:T(8,128)(2,1)} async-done(((bf16[128,2048]{1,0:T(8,128)(2,1)}), bf16[1024,2048]{1,0:T(8,128)(2,1)}) %all-gather.11.cloned.1.call-update) | async-done | bytes 4194320 | tf_op jit(solution)/shard_map/all_gather | solution.py:82
  314.8 5.9 %fusion.4 = bf16[1,512,2048]{2,1,0:T(8,128)(2,1)} fusion(bf16[512,1024]{0,1:T(8,128)(2,1)S(1)} %fusion.10, bf16[1024,2048]{1,0:T(8,128)(2,1)} %all-gather.11.cloned.1.call-done), kind=kOutput, calls=%fused_computation.6 | convolution fusion | flops 2148532224 | bytes 7340032 | tf_op jit(solution)/shard_map/dot_general | solution.py:81
  (36 shorter events, 1.2 us)
Async XLA Ops:
  6.5 184.7 %copy-start = (bf16[1,512,2048]{2,1,0:T(8,128)(2,1)S(1)}, bf16[1,512,2048]{2,1,0:T(8,128)(2,1)}, u32[]{:S(2)}) copy-start(bf16[1,512,2048]{2,1,0:T(8,128)(2,1)} %param.6) | copy-start | bytes 6291460
  6.5 78.7 %all-gather.7.cloned.1.call-start = ((), (), s32[]{:S(2)}) async-start(), calls=%async_computation | async-start | bytes 4718592 | tf_op jit(solution)/shard_map/all_gather | solution.py:31
  7.7 77.6 %copy-start.4 = (f32[1,8,512]{2,1,0:T(8,128)S(1)}, f32[1,8,512]{2,1,0:T(8,128)}, u32[]{:S(2)}) copy-start(f32[1,8,512]{2,1,0:T(8,128)} %param.7) | copy-start | bytes 49156
  9.5 181.7 %all-gather.9.cloned.1.call-start = ((), (), s32[]{:S(2)}) async-start(), calls=%async_computation.1 | async-start | bytes 20971520 | tf_op jit(solution)/shard_map/all_gather | solution.py:32
  85.2 156.7 %all-gather.13.cloned.1.call-start = ((), (), s32[]{:S(2)}) async-start(), calls=%async_computation.3 | async-start | bytes 1310720 | tf_op jit(solution)/shard_map/all_gather | solution.py:57
  203.0 5.1 %copy-start.1 = (f32[4096,512]{1,0:T(8,128)}, f32[4096,512]{1,0:T(8,128)S(1)}, u32[]{:S(2)}) copy-start(f32[4096,512]{1,0:T(8,128)S(1)} %fusion.12) | copy-start | bytes 25165828
  219.1 1.7 copy-start.3
  220.8 2.9 copy-start.6
  223.1 91.7 %all-gather.11.cloned.1.call-start = ((), (), s32[]{:S(2)}) async-start(), calls=%async_computation.2 | async-start | bytes 4718592 | tf_op jit(solution)/shard_map/all_gather | solution.py:82
  243.5 4.9 %copy-start.2 = (f32[512,4,256]{0,2,1:T(8,128)S(1)}, f32[512,4,256]{0,2,1:T(8,128)}, u32[]{:S(2)}) copy-start(f32[512,4,256]{0,2,1:T(8,128)} %fusion.7) | copy-start | bytes 6291460
  243.5 4.9 %copy-start.5 = (f32[1024]{0:T(1024)S(1)}, f32[1024]{0:T(1024)}, u32[]{:S(2)}) copy-start(f32[1024]{0:T(1024)} %param.11) | copy-start | bytes 12292
Sparse Core Ops, SparseCore 0:
  9.7 75.5 all-gather.6
  86.8 104.4 all-gather.8
  223.2 16.6 all-gather.12
  241.9 72.7 all-gather.10
where the time goes:
time: 328 us; the launch traced here: 327 us
  waiting for transfers between devices  246 us (75%)
  matrix products  31.5 us (10%)
  local copies, waits for them, and re-layouts  16.9 us (5%)
  between operations  13.9 us (4%)
  other arithmetic  12.2 us (4%)
  blocking collectives  6.06 us (2%)
    all_gather x1, waiting for transfers between devices, body(): piece = lax.all_gather(full_rows, 'seq', axis=1, tiled=True)  104 us
    all_gather x1, waiting for transfers between devices, body(): full_rows = lax.all_gather(column_slab, 'dp', axis=0, tiled=True)  75.6 us
    all_gather x1, waiting for transfers between devices, body(): lax.all_gather(w_out, 'dp', axis=0, tiled=True)  66 us
    dot_general x1, matrix products, body(): jnp.dot(tok_rows, piece, preferred_element_type=jnp.float32)  11.7 us
    dot_general x1, matrix products, body(): jnp.einsum('hts,shd->thd', weighted, value_rows, preferred_element_type=j...  6.75 us
    reshape x1, local copies, waits for them, and re-layouts, body(): projected = qkv_total.reshape(tok_count, seq_count * qkv_width)  6.59 us
  transfers between devices with their start and end apart: 4, of which 3 were waited for; matrix products, arithmetic and copies ran while one was open for 6% of the time, Pallas kernels for 0%

commit v1 on v0

--- a/solution.py
+++ b/solution.py
@@ -79,7 +79,11 @@
     normed = attended * lax.rsqrt(mean_square + 1e-06) * norm_gain
     gated = (normed * jax.nn.sigmoid(gate_pre)).astype(jnp.bfloat16)
     out_sum = jnp.dot(
-        gated, lax.all_gather(w_out, "dp", axis=0, tiled=True), preferred_element_type=jnp.float32
+        gated,
+        jnp.concatenate(
+            lax.all_to_all(jnp.stack([w_out] * lax.axis_size("dp")), "dp", 0, 0), axis=0
+        ),
+        preferred_element_type=jnp.float32,
     )
     return out_sum.astype(jnp.bfloat16)[None]
 

time: 328 us -> 262 us (0.80)
  waiting for transfers between devices: 246 us -> 173 us
  starting transfers between devices: 0.12 us -> 4.77 us
    all_gather x1 -> x0, waiting for transfers between devices: 66 us -> none  [body(): lax.all_gather(w_out, 'dp', axis=0, tiled=True)]
    all_gather x1, waiting for transfers between devices: 104 us -> 96.8 us  [body(): piece = lax.all_gather(full_rows, 'seq', axis=1, tiled=True)]
    all_to_all x0 -> x1, starting transfers between devices: none -> 4.68 us  [body(): lax.all_to_all(jnp.stack([w_out] * lax.axis_size('dp')), 'dp', 0, 0)]
  transfers between devices with their start and end apart: 4 -> 4, of which waited for: 3 -> 2; matrix products, arithmetic and copies ran while one was open for 6% -> 19% of each run, Pallas kernels for 0% -> 0%
where the time goes in v1:
time: 262 us; the launch traced here: 261 us
  waiting for transfers between devices  173 us (66%)
  matrix products  32.3 us (12%)
  local copies, waits for them, and re-layouts  19.7 us (8%)
  between operations  13.9 us (5%)
  other arithmetic  12 us (5%)
  blocking collectives  6.06 us (2%)
  starting transfers between devices  4.77 us (2%)
    all_gather x1, waiting for transfers between devices, body(): piece = lax.all_gather(full_rows, 'seq', axis=1, tiled=True)  96.8 us
    all_gather x1, waiting for transfers between devices, body(): full_rows = lax.all_gather(column_slab, 'dp', axis=0, tiled=True)  75.6 us
    dot_general x1, matrix products, body(): jnp.dot(tok_rows, piece, preferred_element_type=jnp.float32)  11.7 us
    dot_general x1, matrix products, body(): jnp.dot(gated, jnp.concatenate(lax.all_to_all(jnp.stack([w_out] * lax.axi...  7.55 us
    reshape x1, local copies, waits for them, and re-layouts, body(): projected = qkv_total.reshape(tok_count, seq_count * qkv_width)  6.59 us
    unnamed x1, blocking collectives  6.06 us
    dot_general x1, matrix products, body(): jnp.einsum('hts,shd->thd', weighted, value_rows, preferred_element_type=j...  5.44 us
  transfers between devices with their start and end apart: 4, of which 2 were waited for; matrix products, arithmetic and copies ran while one was open for 19% of the time, Pallas kernels for 0%

profile of v1, /device:TPU:0, one launch (start us, length us, event | category | flops | bytes accessed | tf_op | source)
XLA Modules:
  0.0 261.1 jit_solution(3857105149696081816)
XLA Ops:
  6.5 1.2 constant_dynamic-slice_fusion.2
  7.7 1.0 constant_dynamic-slice_fusion.1
  8.7 0.9 pad_maximum_fusion
  9.6 75.6 %all-gather.6.cloned.1.call-done = bf16[2048,1024]{1,0:T(8,128)(2,1)} async-done(((bf16[256,1024]{1,0:T(8,128)(2,1)}), bf16[2048,1024]{1,0:T(8,128)(2,1)}) %all-gather.6.cloned.1.call-update) | async-done | bytes 4194320 | tf_op jit(solution)/shard_map/all_gather | solution.py:31
  85.3 2.5 stack.2
  87.8 4.7 %all-to-all-start = ((bf16[8,128,2048]{2,1,0:T(8,128)(2,1)}), bf16[8,128,2048]{2,1,0:T(8,128)(2,1)}, u32[]{:S(2)}, u32[]{:S(2)}) async-start(bf16[8,128,2048]{2,1,0:T(8,128)(2,1)} %stack.2), calls=%async_computation | async-start | bytes 8388608 | tf_op jit(solution)/shard_map/all_to_all | solution.py:84
  92.6 1.1 reduce-window.6
  94.0 0.2 fusion.22
  94.5 96.8 %all-gather.8.cloned.1.call-done = bf16[2048,4096]{1,0:T(8,128)(2,1)} async-done(((bf16[2048,1024]{1,0:T(8,128)(2,1)}), bf16[2048,4096]{1,0:T(8,128)(2,1)}) %all-gather.8.cloned.1.call-update) | async-done | bytes 16777232 | tf_op jit(solution)/shard_map/all_gather | solution.py:32
  191.3 11.7 %fusion.9 = f32[4096,512]{1,0:T(8,128)S(1)} fusion(bf16[2048,4096]{1,0:T(8,128)(2,1)} %all-gather.8.cloned.1.call-done, bf16[1,512,2048]{2,1,0:T(8,128)(2,1)S(1)} %copy-done), kind=kOutput, calls=%fused_computation.13 | convolution fusion | flops 8589934592 | bytes 27262976 | tf_op jit(solution)/shard_map/dot_general | solution.py:34
  203.0 3.8 %slice.32 = f32[512,4,768]{0,2,1:T(8,128)} slice(f32[512,4,1024]{0,2,1:T(8,128)S(1)} %bitcast.61), slice={[0:512], [0:4], [0:768]} | slice | bytes 12582912 | tf_op jit(solution)/shard_map/slice | solution.py:37
  206.9 1.3 copy-done.2
  208.2 6.6 %copy.26 = f32[512,3,8,128]{3,0,2,1:T(8,128)} copy(f32[512,3,8,128]{0,3,2,1:T(8,128)} %bitcast.59) | data formatting | bytes 12582912 | tf_op jit(solution)/shard_map/reshape | solution.py:39
  214.7 4.4 %multiply_convert_fusion.1 = bf16[512,3,8,128]{3,0,2,1:T(8,128)(2,1)S(1)} fusion(f32[512,3,8,128]{3,0,2,1:T(8,128)} %copy.26), kind=kLoop, calls=%fused_computation.1 | loop fusion | flops 7864320 | bytes 9437184 | tf_op jit(solution)/shard_map/convert_element_type | solution.py:42
  219.2 1.7 copy-done.3
  220.9 2.3 convolution_convert_fusion
  223.3 0.6 dynamic-slice
  224.5 0.2 dynamic-update-slice
  224.8 6.1 %all-reduce = bf16[32]{0:T(256)(128)(2,1)S(1)} all-reduce(bf16[32]{0:T(256)(128)(2,1)S(1)} %dynamic-update-slice), channel_id=2, replica_groups=mesh['seq'=4,'dp'=8] {'seq'}, use_global_device_ids=true, to_apply=%add | all-reduce | flops 32 | bytes 128
  231.1 3.6 %fusion.7 = f32[512,4,256]{0,2,1:T(8,128)} fusion(f32[512,4,1024]{0,2,1:T(8,128)} %bitcast.62), kind=kLoop, calls=%fused_computation.10 | loop fusion | flops 1572864 | bytes 4194304 | tf_op jit(solution)/shard_map/div | solution.py:80
  234.7 5.4 %fusion = f32[8,128,512]{2,1,0:T(8,128)S(1)} fusion(f32[8,512]{1,0:T(8,128)S(1)} %get-tuple-element.6, pred[512,512]{1,0:T(8,128)(4,1)S(1)} %iota_compare_fusion, bf16[512,3,8,128]{3,0,2,1:T(8,128)(2,1)} %copy-done.3), kind=kOutput, calls=%fused_computation.3 | convolution fusion | flops 1084227584 | bytes 5537792 | tf_op jit(solution)/shard_map/hts,shd->thd/dot_general | solution.py:72
  240.2 1.6 multiply_reduce_fusion
  241.8 5.2 %multiply_reduce_fusion.1 = (f32[512]{0:T(512)S(1)}, f32[8,128,512]{2,1,0:T(8,128)}) fusion(f32[8,128,512]{2,1,0:T(8,128)S(1)} %fusion, f32[8,128,128]{2,1,0:T(8,128)S(1)} %multiply_reduce_fusion, f32[512,8]{0,1:T(8,128)S(1)} %get-tuple-element.5, bf16[512,3,8,128]{3,0,2,1:T(8,128)(2,1)} %copy-done.3), kind=kOutput, calls=%fused_computation.16 | convolution fusion | flops 807927296 | bytes 5785600 | tf_op jit(solution)/shard_map/thd,hde->the/dot_general | solution.py:76
  247.0 7.6 %fusion.4 = bf16[1,512,2048]{2,1,0:T(8,128)(2,1)} fusion(bf16[8,128,2048]{2,1,0:T(8,128)(2,1)} %all-to-all-done, f32[512,8,128]{0,2,1:T(8,128)} %bitcast.60, f32[8,128,512]{2,1,0:T(8,128)} %get-tuple-element.8, f32[8,128]{1,0:T(8,128)S(1)} %bitcast.64, f32[512]{0:T(512)S(1)} %add_rsqrt_fusion), kind=kOutput, calls=%fused_computation.6 | convolution fusion | flops 2150629376 | bytes 10491904 | tf_op jit(solution)/shard_map/dot_general | solution.py:81
  (37 shorter events, 1.0 us)
Async XLA Ops:
  6.5 184.7 %copy-start = (bf16[1,512,2048]{2,1,0:T(8,128)(2,1)S(1)}, bf16[1,512,2048]{2,1,0:T(8,128)(2,1)}, u32[]{:S(2)}) copy-start(bf16[1,512,2048]{2,1,0:T(8,128)(2,1)} %param.6) | copy-start | bytes 6291460
  6.5 78.7 %all-gather.6.cloned.1.call-start = ((), (), s32[]{:S(2)}) async-start(), calls=%async_computation.1 | async-start | bytes 4718592 | tf_op jit(solution)/shard_map/all_gather | solution.py:31
  7.7 77.6 %copy-start.4 = (bf16[128,2048]{1,0:T(8,128)(2,1)S(1)}, bf16[128,2048]{1,0:T(8,128)(2,1)}, u32[]{:S(2)}) copy-start(bf16[128,2048]{1,0:T(8,128)(2,1)} %param.10) | copy-start | bytes 1572868
  9.6 181.7 %all-gather.8.cloned.1.call-start = ((), (), s32[]{:S(2)}) async-start(), calls=%async_computation.2 | async-start | bytes 20971520 | tf_op jit(solution)/shard_map/all_gather | solution.py:32
  87.8 4.7 %copy-start.6 = (f32[1,8,512]{2,1,0:T(8,128)S(1)}, f32[1,8,512]{2,1,0:T(8,128)}, u32[]{:S(2)}) copy-start(f32[1,8,512]{2,1,0:T(8,128)} %param.7) | copy-start | bytes 49156
  87.8 159.2 %all-to-all-start = ((bf16[8,128,2048]{2,1,0:T(8,128)(2,1)}), bf16[8,128,2048]{2,1,0:T(8,128)(2,1)}, u32[]{:S(2)}, u32[]{:S(2)}) async-start(bf16[8,128,2048]{2,1,0:T(8,128)(2,1)} %stack.2), calls=%async_computation | async-start | bytes 8388608 | tf_op jit(solution)/shard_map/all_to_all | solution.py:84
  92.5 147.7 %all-gather.10.cloned.1.call-start = ((), (), s32[]{:S(2)}) async-start(), calls=%async_computation.3 | async-start | bytes 1310720 | tf_op jit(solution)/shard_map/all_gather | solution.py:57
  203.0 5.1 %copy-start.2 = (f32[4096,512]{1,0:T(8,128)}, f32[4096,512]{1,0:T(8,128)S(1)}, u32[]{:S(2)}) copy-start(f32[4096,512]{1,0:T(8,128)S(1)} %fusion.9) | copy-start | bytes 25165828
  219.2 1.8 copy-start.3
  220.9 2.3 copy-start.7
  241.8 5.3 %copy-start.5 = (f32[1024]{0:T(1024)S(1)}, f32[1024]{0:T(1024)}, u32[]{:S(2)}) copy-start(f32[1024]{0:T(1024)} %param.11) | copy-start | bytes 12292
  247.0 7.6 %copy-start.1 = (bf16[1,512,2048]{2,1,0:T(8,128)(2,1)S(1)}, bf16[1,512,2048]{2,1,0:T(8,128)(2,1)}, u32[]{:S(2)}) copy-start(bf16[1,512,2048]{2,1,0:T(8,128)(2,1)} %param.6) | copy-start | bytes 6291460
Sparse Core Ops, SparseCore 0:
  9.7 75.5 all-gather.5
  86.8 104.4 all-gather.7
  223.4 16.6 all-gather.9
